TPU v7x, 128 devices: a whole 4x4x4 slice. The times are simulated.
128 devices in a mesh: row: 8 (over z_hi, y), col: 16 (over x, z_lo, core).
Axes of the slice: x: 4, y: 4, z: 4 (z_hi: 2, z_lo: 2; z = z_hi * 2 + z_lo), core: 2. Of those that a mesh axis runs over, the one named last changes fastest.
Arguments:
- positions: float32 [3, 16384], P(None, ('row', 'col')), may hold values from 0 to 5
- species: int32 [16384], P(('row', 'col')), may hold values from 0 to 99
- tile_list: int32 [8, 16, 2, 3], P('row', 'col'), may hold values from 0 to 15, as said below
- pair_mask: int32 [8, 16, 2, 128, 128], P('row', 'col'), may hold values 0 or 1
- embed: float32 [100, 128], replicated, may hold values from -6 to 6
- w_in: float32 [2, 128, 128], replicated, may hold values from -0.5 to 0.5
- rbf_weight: bfloat16 [2, 256, 128], replicated, may hold values from -1 to 1
- rbf_bias: float32 [2, 128], replicated, may hold values from -4 to 4
- filt_weight: bfloat16 [2, 128, 128], replicated, may hold values from -1 to 1
- w_update1: float32 [2, 128, 128], replicated, may hold values from -1 to 1
- w_update2: float32 [2, 128, 128], replicated, may hold values from -0.5 to 0.5
- w_out1: float32 [128, 64], replicated, may hold values from -0.5 to 0.5
- w_out2: float32 [64], replicated, may hold values from -0.75 to 0.75
Outputs:
- atom_energy: float32 [16384], P(('row', 'col'))
- forces: float32 [3, 16384], P(None, ('row', 'col'))
Inputs may be any that keep to these rules, and one draw needn't show every extreme that they name: `tile_list`: A live slot (flag 1) names a row block below 16 and a column block below 8; the live slots of one device name distinct row blocks and come first; a dead slot is all zeros; every device has at least one live slot and some device has all 2.
All inputs are finite; a program needn't handle non-finite values. No bound on the sum of `pair_mask` on one device may be relied on, other than what follows from the above.
Results may differ from a plain program's by a relative error of at most 0.007.
Values sent between devices are 32-bit elements; how exact they have to be, the bound alone decides.
No kernel may reach another device: no remote copies, remote signals or barrier semaphores. Data moves between devices by JAX's collectives and lax.ppermute only.
A program may use at most 192 MiB of HBM per device.

v0:
```python
from functools import partial
import math
import jax
import jax.numpy as jnp
from jax import lax
from jax.sharding import PartitionSpec as P

LAYERS = 2
CUTOFF = 5.0
NORM_DIV = 4.0
HIGH = lax.Precision.HIGHEST


def shifted_softplus(values):
    return jax.nn.softplus(values) - math.log(2.0)


def tile_message(row_coord, col_coord, col_feat, pair_gate, rbf_w, rbf_b, filt_w):
    offset = row_coord[:, :, None] - col_coord[:, None, :]
    distance = jnp.sqrt(jnp.sum(offset * offset, axis=0) + 0.01)
    n_gauss = rbf_w.shape[0]
    rows_here = distance.shape[0]
    feat_width = filt_w.shape[1]
    centers = jnp.arange(n_gauss).astype(distance.dtype) * (CUTOFF / n_gauss)
    sharpness = (n_gauss / CUTOFF) ** 2 / 32.0
    expand = jnp.exp(-sharpness * (distance[:, :, None] - centers) ** 2).astype(jnp.bfloat16)
    pre_act = (
        jnp.dot(
            expand.reshape(rows_here * rows_here, n_gauss),
            rbf_w,
            preferred_element_type=jnp.float32,
        )
        + rbf_b
    )
    hidden = shifted_softplus(pre_act).astype(jnp.bfloat16)
    filters = jnp.dot(hidden, filt_w, preferred_element_type=jnp.float32).reshape(
        rows_here, rows_here, feat_width
    )
    envelope = jnp.where(distance < CUTOFF, 0.5 * (jnp.cos(math.pi * distance / CUTOFF) + 1.0), 0.0)
    envelope = envelope * pair_gate.astype(distance.dtype)
    return jnp.einsum("ijf,ij,jf->if", filters, envelope, col_feat) / NORM_DIV


def atom_update(message, w_one, w_two):
    return jnp.dot(shifted_softplus(jnp.dot(message, w_one, precision=HIGH)), w_two, precision=HIGH)


def energy_head(features, w_out1, w_out2):
    return jnp.dot(
        shifted_softplus(jnp.dot(features, w_out1, precision=HIGH)), w_out2, precision=HIGH
    )


def add_rows(target, addend, start, dim_index):
    current = lax.dynamic_slice_in_dim(target, start, addend.shape[dim_index], dim_index)
    return lax.dynamic_update_slice_in_dim(target, current + addend, start, dim_index)


def body(
    positions,
    species,
    tile_list,
    pair_mask,
    embed,
    w_in,
    rbf_weight,
    rbf_bias,
    filt_weight,
    w_update1,
    w_update2,
    w_out1,
    w_out2,
):
    block_len = positions.shape[1]
    feat_width = embed.shape[1]
    slot_count = tile_list.shape[2]
    n_rowdev = lax.axis_size("row")
    n_coldev = lax.axis_size("col")
    table = tile_list.reshape(slot_count, 3)
    gates = pair_mask.reshape(slot_count, block_len, block_len) * table[:, 2][:, None, None]
    row_coords = lax.all_gather(positions, "col", axis=1, tiled=True)
    onehot = (species[:, None] == jnp.arange(embed.shape[0], dtype=jnp.int32)[None, :]).astype(
        jnp.float32
    )
    features = jnp.dot(onehot, embed, precision=HIGH)
    saved = []
    for layer_idx in range(LAYERS):
        mixed_in = jnp.dot(features, w_in[layer_idx], precision=HIGH)
        col_feats, col_coords = (
            lax.all_gather(mixed_in, "row", axis=0, tiled=True),
            lax.all_gather(positions, "row", axis=1, tiled=True),
        )
        partial_sum = jnp.zeros((n_coldev * block_len, feat_width), jnp.float32)
        pullbacks = []
        for slot_idx in range(slot_count):
            row_start = table[slot_idx, 0] * block_len
            col_start = table[slot_idx, 1] * block_len
            row_piece = lax.dynamic_slice_in_dim(row_coords, row_start, block_len, 1)
            col_piece = lax.dynamic_slice_in_dim(col_coords, col_start, block_len, 1)
            feat_piece = lax.dynamic_slice_in_dim(col_feats, col_start, block_len, 0)
            local_fn = partial(
                tile_message,
                pair_gate=gates[slot_idx],
                rbf_w=rbf_weight[layer_idx],
                rbf_b=rbf_bias[layer_idx],
                filt_w=filt_weight[layer_idx],
            )
            message_part = local_fn(row_piece, col_piece, feat_piece)
            partial_sum = add_rows(partial_sum, message_part, row_start, 0)
        message = lax.psum_scatter(partial_sum, "col", scatter_dimension=0, tiled=True)
        update_fn = partial(atom_update, w_one=w_update1[layer_idx], w_two=w_update2[layer_idx])
        update_value, update_pull = jax.vjp(update_fn, message)
        saved.append((col_feats, col_coords, pullbacks, update_pull))
        features = features + update_value

    def head_fn(current_feats):
        return energy_head(current_feats, w_out1, w_out2)

    energies, head_pull = jax.vjp(head_fn, features)
    grad_feat = head_pull(jnp.ones_like(energies))[0]
    row_force = jnp.zeros((3, n_coldev * block_len), jnp.float32)
    col_force = jnp.zeros((3, block_len), jnp.float32)
    for layer_idx in reversed(range(LAYERS)):
        col_feats, col_coords, pullbacks, update_pull = saved[layer_idx]
        grad_msg = update_pull(grad_feat)[0]
        grad_rows = lax.all_gather(grad_msg, "col", axis=0, tiled=True)
        grad_colx = jnp.zeros((n_rowdev * block_len, feat_width), jnp.float32)
        grad_colpos = jnp.zeros((3, n_rowdev * block_len), jnp.float32)
        for slot_idx in range(slot_count):
            row_start = table[slot_idx, 0] * block_len
            col_start = table[slot_idx, 1] * block_len
            cotangent = lax.dynamic_slice_in_dim(grad_rows, row_start, block_len, 0)
            row_piece = lax.dynamic_slice_in_dim(row_coords, row_start, block_len, 1)
            col_piece = lax.dynamic_slice_in_dim(col_coords, col_start, block_len, 1)
            feat_piece = lax.dynamic_slice_in_dim(col_feats, col_start, block_len, 0)
            local_fn = partial(
                tile_message,
                pair_gate=gates[slot_idx],
                rbf_w=rbf_weight[layer_idx],
                rbf_b=rbf_bias[layer_idx],
                filt_w=filt_weight[layer_idx],
            )
            unused_out, pullback = jax.vjp(local_fn, row_piece, col_piece, feat_piece)
            grad_rowp, grad_colp, grad_feats = pullback(cotangent)
            row_force = add_rows(row_force, grad_rowp, row_start, 1)
            grad_colpos = add_rows(grad_colpos, grad_colp, col_start, 1)
            grad_colx = add_rows(grad_colx, grad_feats, col_start, 0)
        grad_inputs, grad_cpos = (
            lax.psum_scatter(grad_colx, "row", scatter_dimension=0, tiled=True),
            lax.psum_scatter(grad_colpos, "row", scatter_dimension=1, tiled=True),
        )
        col_force = col_force + grad_cpos
        grad_feat = grad_feat + jnp.dot(grad_inputs, w_in[layer_idx].T, precision=HIGH)
    own_rows = lax.psum_scatter(row_force, "col", scatter_dimension=1, tiled=True)
    forces = -(own_rows + col_force)
    return (energies, forces)


def solution(mesh):
    return jax.shard_map(
        body,
        mesh=mesh,
        in_specs=(
            P(None, ("row", "col")),
            P(("row", "col")),
            P("row", "col", None, None),
            P("row", "col", None, None, None),
            P(),
            P(),
            P(),
            P(),
            P(),
            P(),
            P(),
            P(),
            P(),
        ),
        out_specs=(P(("row", "col")), P(None, ("row", "col"))),
        check_vma=False,
    )
```

profile of v0, /device:TPU:0, one launch (start us, length us, event | category | flops | bytes accessed | tf_op | source)
XLA Modules:
  0.0 683.8 jit_solution(805372431139413703)
XLA Ops:
  11.1 20.5 %all_gather.19 = f32[3,2048]{1,0:T(4,128)S(1)} all-gather(f32[3,128]{1,0:T(4,128)} %param.15), channel_id=1, replica_groups=mesh['row'=8,'col'=16] {'col'}, dimensions={1}, use_global_device_ids=true | all-gather | bytes 26112 | tf_op jit(solution)/shard_map/all_gather | solution.py:81
  31.6 31.0 %all_gather.20 = f32[3,1024]{1,0:T(4,128)S(1)} all-gather(f32[3,128]{1,0:T(4,128)} %param.15), channel_id=1, replica_groups=mesh['row'=8,'col'=16] {'row'}, dimensions={1}, use_global_device_ids=true | all-gather | bytes 13824 | tf_op jit(solution)/shard_map/all_gather | solution.py:91
  66.2 35.0 %all_gather.21 = f32[1024,128]{1,0:T(8,128)S(1)} all-gather(f32[128,128]{1,0:T(8,128)S(1)} %fusion.108), channel_id=1, replica_groups=mesh['row'=8,'col'=16] {'row'}, dimensions={0}, use_global_device_ids=true | all-gather | bytes 589824 | tf_op jit(solution)/shard_map/all_gather | solution.py:90
  103.2 10.9 %add_convert_fusion.3 = (bf16[16384,128]{1,0:T(8,128)(2,1)S(1)}, f32[16384,128]{1,0:T(8,128)}) fusion(f32[128]{0:T(128)S(1)} %get-tuple-element.65, bf16[2,256,128]{2,1,0:T(8,128)(2,1)} %param.21, f32[256]{0:T(256)S(1)} %convert_multiply_fusion, f32[16384]{0:T(1024)S(1)} %get-tuple-element.54), kind=kOutput, calls=%fused_computation.93 | convolution fusion | flops 1109393408 | bytes 12715520 | tf_op jit(solution)/shard_map/dot_general | solution.py:28
  120.7 10.1 %add_convert_fusion.2 = (bf16[16384,128]{1,0:T(8,128)(2,1)S(1)}, f32[16384,128]{1,0:T(8,128)}) fusion(f32[128]{0:T(128)S(1)} %get-tuple-element.65, bf16[2,256,128]{2,1,0:T(8,128)(2,1)S(1)} %copy-done.24, f32[16384]{0:T(1024)S(1)} %get-tuple-element.59, f32[256]{0:T(256)S(1)} %convert_multiply_fusion), kind=kOutput, calls=%fused_computation.90 | convolution fusion | flops 1109393408 | bytes 12715520 | tf_op jit(solution)/shard_map/dot_general | solution.py:28
  138.7 11.3 %add_convert_fusion.1 = (bf16[16384,128]{1,0:T(8,128)(2,1)}, f32[16384,128]{1,0:T(8,128)}) fusion(f32[128]{0:T(128)S(1)} %get-tuple-element.64, bf16[2,256,128]{2,1,0:T(8,128)(2,1)S(1)} %copy-done.24, f32[256]{0:T(256)S(1)} %convert_multiply_fusion, f32[16384]{0:T(1024)S(1)} %get-tuple-element.54), kind=kOutput, calls=%fused_computation.89 | convolution fusion | flops 1109393408 | bytes 12715520 | tf_op jit(solution)/shard_map/dot_general | solution.py:28
  150.1 11.4 %add_convert_fusion = (bf16[16384,128]{1,0:T(8,128)(2,1)}, f32[16384,128]{1,0:T(8,128)}) fusion(f32[128]{0:T(128)S(1)} %get-tuple-element.64, bf16[2,256,128]{2,1,0:T(8,128)(2,1)S(1)} %copy-done.24, f32[16384]{0:T(1024)S(1)} %get-tuple-element.59, f32[256]{0:T(256)S(1)} %convert_multiply_fusion), kind=kOutput, calls=%fused_computation.88 | convolution fusion | flops 1109393408 | bytes 12715520 | tf_op jit(solution)/shard_map/dot_general | solution.py:28
  161.5 36.1 %reduce-scatter.10.cloned.1.call-done = f32[128,128]{0,1:T(8,128)} async-done(((f32[2048,128]{0,1:T(8,128)}), f32[128,128]{0,1:T(8,128)}) %reduce-scatter.10.cloned.1.call-update) | async-done | bytes 65552 | tf_op jit(solution)/shard_map/reduce_scatter | solution.py:110
  199.2 35.3 %all_gather.22 = f32[1024,128]{1,0:T(8,128)S(1)} all-gather(f32[128,128]{1,0:T(8,128)S(1)} %fusion.95), channel_id=1, replica_groups=mesh['row'=8,'col'=16] {'row'}, dimensions={0}, use_global_device_ids=true | all-gather | bytes 589824 | tf_op jit(solution)/shard_map/all_gather | solution.py:90
  234.5 6.9 %multiply_reduce_fusion.3 = (f32[128,128]{0,1:T(8,128)S(1)}, f32[128,128,128]{2,1,0:T(8,128)}) fusion(f32[128,128]{0,1:T(8,128)S(1)} %get-tuple-element.43, f32[128,128]{1,0:T(8,128)S(1)} %get-tuple-element.53, bf16[128,128,128]{2,1,0:T(8,128)(2,1)} %bitcast.250, bf16[2,128,128]{2,1,0:T(8,128)(2,1)S(1)} %copy-done.13), kind=kOutput, calls=%fused_computation.85 | convolution fusion | flops 543145984 | bytes 12812288 | tf_op jit(solution)/shard_map/dot_general | solution.py:36
  250.1 60.0 %reduce-scatter.12.cloned.1.call-done = f32[128,128]{0,1:T(8,128)} async-done(((f32[2048,128]{0,1:T(8,128)}), f32[128,128]{0,1:T(8,128)}) %reduce-scatter.12.cloned.1.call-update) | async-done | bytes 65552 | tf_op jit(solution)/shard_map/reduce_scatter | solution.py:110
  313.4 31.0 %all-gather.3.cloned.1.call-done = f32[2048,128]{1,0:T(8,128)} async-done(((f32[128,128]{1,0:T(8,128)}), f32[2048,128]{1,0:T(8,128)}) %all-gather.3.cloned.1.call-update) | async-done | bytes 1048592 | tf_op jit(solution)/shard_map/all_gather | solution.py:126
  356.7 71.7 %reduce-scatter.14.cloned.1.call-done = f32[128,128]{1,0:T(8,128)} async-done(((f32[1024,128]{1,0:T(8,128)}), f32[128,128]{1,0:T(8,128)}) %reduce-scatter.14.cloned.1.call-update) | async-done | bytes 65552 | tf_op jit(solution)/shard_map/reduce_scatter | solution.py:149
  442.1 19.9 %all-gather.5.cloned.1.call-done = f32[2048,128]{1,0:T(8,128)} async-done(((f32[128,128]{1,0:T(8,128)}), f32[2048,128]{1,0:T(8,128)}) %all-gather.5.cloned.1.call-update) | async-done | bytes 1048592 | tf_op jit(solution)/shard_map/all_gather | solution.py:126
  465.9 9.3 %fusion.17 = bf16[16384,128]{1,0:T(8,128)(2,1)S(1)} fusion(bf16[16384,128]{1,0:T(8,128)(2,1)S(1)} %bitcast.256, f32[16384,128]{1,0:T(8,128)} %get-tuple-element.79, bf16[2,128,128]{2,1,0:T(8,128)(2,1)S(1)} %copy-done.13), kind=kOutput, calls=%fused_computation.45 | convolution fusion | flops 566231040 | bytes 16809984 | tf_op jit(solution)/shard_map/transpose(jvp())/dot_general | solution.py:36
  475.3 7.1 %fusion.26 = f32[16384]{0:T(1024)S(1)} fusion(f32[256]{0:T(256)S(1)} %convert_multiply_fusion, f32[16384]{0:T(1024)S(1)} %get-tuple-element.54, bf16[16384,128]{1,0:T(8,128)(2,1)S(1)} %fusion.17, bf16[2,256,128]{2,1,0:T(8,128)(2,1)S(1)} %copy-done.24), kind=kOutput, calls=%fused_computation.54 | convolution fusion | flops 1111474176 | bytes 4391936 | tf_op jit(solution)/shard_map/transpose(jvp())/dot_general | solution.py:28
  482.4 7.1 %fusion.21 = bf16[16384,128]{1,0:T(8,128)(2,1)S(1)} fusion(bf16[16384,128]{1,0:T(8,128)(2,1)S(1)} %bitcast.254, f32[16384,128]{1,0:T(8,128)S(1)} %bitcast.264, bf16[2,128,128]{2,1,0:T(8,128)(2,1)S(1)} %copy-done.13), kind=kOutput, calls=%fused_computation.49 | convolution fusion | flops 566231040 | bytes 16809984 | tf_op jit(solution)/shard_map/transpose(jvp())/dot_general | solution.py:36
  489.5 7.3 %fusion.27 = f32[16384]{0:T(1024)S(1)} fusion(f32[256]{0:T(256)S(1)} %convert_multiply_fusion, f32[16384]{0:T(1024)S(1)} %get-tuple-element.54, bf16[16384,128]{1,0:T(8,128)(2,1)S(1)} %fusion.21, bf16[2,256,128]{2,1,0:T(8,128)(2,1)S(1)} %copy-done.24), kind=kOutput, calls=%fused_computation.55 | convolution fusion | flops 1111474176 | bytes 4391936 | tf_op jit(solution)/shard_map/transpose(jvp())/dot_general | solution.py:28
  504.4 9.2 %fusion.23 = bf16[16384,128]{1,0:T(8,128)(2,1)S(1)} fusion(bf16[16384,128]{1,0:T(8,128)(2,1)S(1)} %bitcast.255, f32[16384,128]{1,0:T(8,128)} %get-tuple-element.75, bf16[2,128,128]{2,1,0:T(8,128)(2,1)S(1)} %copy-done.13), kind=kOutput, calls=%fused_computation.51 | convolution fusion | flops 566231040 | bytes 16809984 | tf_op jit(solution)/shard_map/transpose(jvp())/dot_general | solution.py:36
  513.6 7.3 %fusion.25 = f32[16384]{0:T(1024)S(1)} fusion(f32[16384]{0:T(1024)S(1)} %get-tuple-element.59, f32[256]{0:T(256)S(1)} %convert_multiply_fusion, bf16[16384,128]{1,0:T(8,128)(2,1)S(1)} %fusion.23, bf16[2,256,128]{2,1,0:T(8,128)(2,1)S(1)} %copy-done.24), kind=kOutput, calls=%fused_computation.53 | convolution fusion | flops 1111474176 | bytes 4391936 | tf_op jit(solution)/shard_map/transpose(jvp())/dot_general | solution.py:28
  520.9 9.2 %fusion.19 = bf16[16384,128]{1,0:T(8,128)(2,1)S(1)} fusion(bf16[16384,128]{1,0:T(8,128)(2,1)S(1)} %bitcast.253, f32[16384,128]{1,0:T(8,128)} %get-tuple-element.83, bf16[2,128,128]{2,1,0:T(8,128)(2,1)S(1)} %copy-done.13), kind=kOutput, calls=%fused_computation.47 | convolution fusion | flops 566231040 | bytes 16809984 | tf_op jit(solution)/shard_map/transpose(jvp())/dot_general | solution.py:36
  530.2 7.1 %fusion.24 = f32[16384]{0:T(1024)S(1)} fusion(f32[16384]{0:T(1024)S(1)} %get-tuple-element.59, f32[256]{0:T(256)S(1)} %convert_multiply_fusion, bf16[16384,128]{1,0:T(8,128)(2,1)S(1)} %fusion.19, bf16[2,256,128]{2,1,0:T(8,128)(2,1)S(1)} %copy-done.24), kind=kOutput, calls=%fused_computation.52 | convolution fusion | flops 1111474176 | bytes 4391936 | tf_op jit(solution)/shard_map/transpose(jvp())/dot_general | solution.py:28
  541.9 69.4 %reduce-scatter.18.cloned.1.call-done = f32[128,3]{1,0:T(8,128)} async-done(((f32[1024,3]{1,0:T(8,128)}), f32[128,3]{1,0:T(8,128)}) %reduce-scatter.18.cloned.1.call-update) | async-done | bytes 1552
  612.2 62.9 %reduce-scatter.16.cloned.1.call-done = f32[128,3]{1,0:T(8,128)} async-done(((f32[2048,3]{1,0:T(8,128)}), f32[128,3]{1,0:T(8,128)}) %reduce-scatter.16.cloned.1.call-update) | async-done | bytes 1552
  (153 shorter events, 79.0 us)
Async XLA Ops:
  7.2 57.1 %copy-start = (f32[100,128]{1,0:T(8,128)S(1)}, f32[100,128]{1,0:T(8,128)}, u32[]{:S(2)}) copy-start(f32[100,128]{1,0:T(8,128)} %param.19) | copy-start | bytes 153604
  7.2 190.4 %reduce-scatter.10.cloned.1.call-start = ((), (), s32[]{:S(2)}) async-start(), calls=%async_computation.5 | async-start | bytes 1114112 | tf_op jit(solution)/shard_map/reduce_scatter | solution.py:110
  101.2 12.9 %copy-start.16 = (f32[3,128]{1,0:T(4,128)}, f32[3,128]{1,0:T(4,128)S(1)}, u32[]{:S(2)}) copy-start(f32[3,128]{1,0:T(4,128)S(1)} %get-tuple-element.62) | copy-start | bytes 4612
  101.2 12.9 %copy-start.20 = (f32[3,128]{1,0:T(4,128)}, f32[3,128]{1,0:T(4,128)S(1)}, u32[]{:S(2)}) copy-start(f32[3,128]{1,0:T(4,128)S(1)} %get-tuple-element.63) | copy-start | bytes 4612
  101.3 12.8 %copy-start.18 = (f32[3,128]{1,0:T(4,128)}, f32[3,128]{1,0:T(4,128)S(1)}, u32[]{:S(2)}) copy-start(f32[3,128]{1,0:T(4,128)S(1)} %get-tuple-element.60) | copy-start | bytes 4612
  101.3 12.8 %copy-start.22 = (f32[3,128]{1,0:T(4,128)}, f32[3,128]{1,0:T(4,128)S(1)}, u32[]{:S(2)}) copy-start(f32[3,128]{1,0:T(4,128)S(1)} %get-tuple-element.61) | copy-start | bytes 4612
  103.2 10.9 %copy-start.13 = (bf16[2,128,128]{2,1,0:T(8,128)(2,1)S(1)}, bf16[2,128,128]{2,1,0:T(8,128)(2,1)}, u32[]{:S(2)}) copy-start(bf16[2,128,128]{2,1,0:T(8,128)(2,1)} %param.23) | copy-start | bytes 196612
  138.5 171.7 %reduce-scatter.12.cloned.1.call-start = ((), (), s32[]{:S(2)}) async-start(), calls=%async_computation.6 | async-start | bytes 1114112 | tf_op jit(solution)/shard_map/reduce_scatter | solution.py:110
  150.1 47.5 %copy-start.11 = (f32[2,128,128]{2,1,0:T(8,128)S(1)}, f32[2,128,128]{2,1,0:T(8,128)}, u32[]{:S(2)}) copy-start(f32[2,128,128]{2,1,0:T(8,128)} %param.24) | copy-start | bytes 393220
  150.1 48.7 %copy-start.14 = (f32[2,128,128]{2,1,0:T(8,128)S(1)}, f32[2,128,128]{2,1,0:T(8,128)}, u32[]{:S(2)}) copy-start(f32[2,128,128]{2,1,0:T(8,128)} %param.25) | copy-start | bytes 393220
  150.1 48.9 %copy-start.12 = (f32[2,128,128]{2,1,0:T(8,128)S(1)}, f32[2,128,128]{2,1,0:T(8,128)}, u32[]{:S(2)}) copy-start(f32[2,128,128]{2,1,0:T(8,128)} %param.20) | copy-start | bytes 393220
  241.4 70.1 %copy-start.15 = (f32[128,64]{0,1:T(8,128)S(1)}, f32[128,64]{0,1:T(8,128)}, u32[]{:S(2)}) copy-start(f32[128,64]{0,1:T(8,128)} %param.26) | copy-start | bytes 98308
  241.4 70.4 %copy-start.25 = (f32[64]{0:T(128)S(1)}, f32[64]{0:T(128)}, u32[]{:S(2)}) copy-start(f32[64]{0:T(128)} %param.27) | copy-start | bytes 772
  249.7 94.7 %all-gather.3.cloned.1.call-start = ((), (), s32[]{:S(2)}) async-start(), calls=%async_computation.7 | async-start | bytes 1114112 | tf_op jit(solution)/shard_map/all_gather | solution.py:126
  313.4 115.0 %reduce-scatter.14.cloned.1.call-start = ((), (), s32[]{:S(2)}) async-start(), calls=%async_computation.8 | async-start | bytes 589824 | tf_op jit(solution)/shard_map/reduce_scatter | solution.py:149
  356.7 105.3 %all-gather.5.cloned.1.call-start = ((), (), s32[]{:S(2)}) async-start(), calls=%async_computation.9 | async-start | bytes 1114112 | tf_op jit(solution)/shard_map/all_gather | solution.py:126
  430.7 180.6 %reduce-scatter.18.cloned.1.call-start = ((), (), s32[]{:S(2)}) async-start(), calls=%async_computation.11 | async-start | bytes 589824
  462.8 19.5 %slice-start.4 = ((s8[8388608]{0:T(1024)(128)(4,1)}), s8[4194304]{0:T(1024)(128)(4,1)S(1)}, s32[]{:S(2)}) async-start(s8[8388608]{0:T(1024)(128)(4,1)} %bitcast.263), calls=%async_computation.16 | async-start | bytes 8388608
  465.9 16.5 %slice-start.5 = ((s8[8388608]{0:T(1024)(128)(4,1)}), s8[4194304]{0:T(1024)(128)(4,1)S(1)}, s32[]{:S(2)}) async-start(s8[8388608]{0:T(1024)(128)(4,1)} %bitcast.263), calls=%async_computation.17 | async-start | bytes 8388608
  475.2 21.6 %slice-start = ((s8[8388608]{0:T(1024)(128)(4,1)}), s8[4194304]{0:T(1024)(128)(4,1)S(1)}, s32[]{:S(2)}) async-start(s8[8388608]{0:T(1024)(128)(4,1)} %bitcast.245), calls=%async_computation.12 | async-start | bytes 8388608
  482.4 14.5 %slice-start.1 = ((s8[8388608]{0:T(1024)(128)(4,1)}), s8[4194304]{0:T(1024)(128)(4,1)S(1)}, s32[]{:S(2)}) async-start(s8[8388608]{0:T(1024)(128)(4,1)} %bitcast.245), calls=%async_computation.13 | async-start | bytes 8388608
  530.2 8.1 %copy-start.17 = (f32[3,128]{1,0:T(4,128)S(1)}, f32[3,128]{1,0:T(4,128)}, u32[]{:S(2)}) copy-start(f32[3,128]{1,0:T(4,128)} %copy-done.16) | copy-start | bytes 4612
  530.2 146.4 %copy-start.1 = (f32[100,128]{1,0:T(8,128)S(1)}, f32[100,128]{1,0:T(8,128)}, u32[]{:S(2)}) copy-start(f32[100,128]{1,0:T(8,128)} %param.19) | copy-start | bytes 153604
  539.7 135.4 %reduce-scatter.16.cloned.1.call-start = ((), (), s32[]{:S(2)}) async-start(), calls=%async_computation.10 | async-start | bytes 1114112
  (15 other events, 66.4 us)
Sparse Core Ops, SparseCore 0:
  138.6 58.9 reduce-scatter.9
  249.8 60.3 reduce-scatter.11
  313.5 30.8 all-gather.2
  356.8 71.5 reduce-scatter.13
  430.8 31.0 all-gather.4
  539.8 71.4 reduce-scatter.17
  613.7 61.3 reduce-scatter.15
where the time goes:
time: 692 us; the launch traced here: 684 us
  waiting for transfers between devices  351 us (51%)
  matrix products  144 us (21%)
  blocking collectives  122 us (18%)
  other arithmetic  37.7 us (5%)
  between operations  17.9 us (3%)
  local copies, waits for them, and re-layouts  10.9 us (2%)
    unnamed x9, waiting for transfers between devices  132 us
    reduce_scatter x2, waiting for transfers between devices, body(): lax.psum_scatter(partial_sum, 'col', scatter_dimension=0, tiled=True)  96.2 us
    dot_general x8, matrix products, tile_message(): jnp.dot(expand.reshape(rows_here * rows_here, n_gauss), rbf_w, preferred_...  72.5 us
    reduce_scatter x1, waiting for transfers between devices, body(): lax.psum_scatter(grad_colx, 'row', scatter_dimension=0, tiled=True)  71.7 us
    all_gather x2, blocking collectives, body(): lax.all_gather(mixed_in, 'row', axis=0, tiled=True)  70.3 us
    dot_general x8, matrix products, tile_message(): jnp.dot(hidden, filt_w, preferred_element_type=jnp.float32)  61.5 us
    all_gather x2, waiting for transfers between devices, body(): grad_rows = lax.all_gather(grad_msg, 'col', axis=0, tiled=True)  50.8 us
    dot_general x8, other arithmetic, tile_message(): return jnp.einsum('ijf,ij,jf->if', filters, envelope, col_feat) / NORM_DIV  32.3 us
  transfers between devices with their start and end apart: 7, of which 7 were waited for; matrix products, arithmetic and copies ran while one was open for 5% of the time, Pallas kernels for 0%

commit v1 on v0

--- a/solution.py
+++ b/solution.py
@@ -87,7 +87,9 @@
     for layer_idx in range(LAYERS):
         mixed_in = jnp.dot(features, w_in[layer_idx], precision=HIGH)
         col_feats, col_coords = (
-            lax.all_gather(mixed_in, "row", axis=0, tiled=True),
+            jnp.concatenate(
+                lax.all_to_all(jnp.stack([mixed_in] * lax.axis_size("row")), "row", 0, 0), axis=0
+            ),
             lax.all_gather(positions, "row", axis=1, tiled=True),
         )
         partial_sum = jnp.zeros((n_coldev * block_len, feat_width), jnp.float32)

time: 692 us -> 657 us (0.949)
  blocking collectives: 122 us -> 50.8 us
  starting transfers between devices: 0.91 us -> 15.2 us
  waiting for transfers between devices: 351 us -> 363 us
    all_gather x2 -> x0, blocking collectives: 70.3 us -> none  [body(): lax.all_gather(mixed_in, 'row', axis=0, tiled=True)]
    all_to_all x0 -> x2, starting transfers between devices: none -> 14.5 us  [body(): lax.all_to_all(jnp.stack([mixed_in] * lax.axis_size('row')), 'row', 0, 0)]
    reduce_scatter x2, waiting for transfers between devices: 96.2 us -> 108 us  [body(): lax.psum_scatter(partial_sum, 'col', scatter_dimension=0, tiled=True)]
  transfers between devices with their start and end apart: 7 -> 9, of which waited for: 7 -> 7; matrix products, arithmetic and copies ran while one was open for 5% -> 10% of each run, Pallas kernels for 0% -> 0%
where the time goes in v1:
time: 657 us; the launch traced here: 647 us
  waiting for transfers between devices  363 us (55%)
  matrix products  147 us (22%)
  blocking collectives  50.8 us (8%)
  other arithmetic  37.7 us (6%)
  between operations  18 us (3%)
  starting transfers between devices  15.2 us (2%)
  local copies, waits for them, and re-layouts  14.4 us (2%)
    unnamed x9, waiting for transfers between devices  132 us
    reduce_scatter x2, waiting for transfers between devices, body(): lax.psum_scatter(partial_sum, 'col', scatter_dimension=0, tiled=True)  108 us
    dot_general x8, matrix products, tile_message(): jnp.dot(expand.reshape(rows_here * rows_here, n_gauss), rbf_w, preferred_...  75.4 us
    reduce_scatter x1, waiting for transfers between devices, body(): lax.psum_scatter(grad_colx, 'row', scatter_dimension=0, tiled=True)  71.7 us
    dot_general x8, matrix products, tile_message(): jnp.dot(hidden, filt_w, preferred_element_type=jnp.float32)  62.5 us
    all_gather x2, waiting for transfers between devices, body(): grad_rows = lax.all_gather(grad_msg, 'col', axis=0, tiled=True)  50.7 us
    dot_general x8, other arithmetic, tile_message(): return jnp.einsum('ijf,ij,jf->if', filters, envelope, col_feat) / NORM_DIV  32.3 us
    all_gather x1, blocking collectives, body(): lax.all_gather(positions, 'row', axis=1, tiled=True)  31.3 us
  transfers between devices with their start and end apart: 9, of which 7 were waited for; matrix products, arithmetic and copies ran while one was open for 10% of the time, Pallas kernels for 0%

profile of v1, /device:TPU:0, one launch (start us, length us, event | category | flops | bytes accessed | tf_op | source)
XLA Modules:
  0.0 646.6 jit_solution(7162189615139306238)
XLA Ops:
  10.8 7.9 %all-to-all-start = ((f32[8,128,128]{2,1,0:T(8,128)}), f32[8,128,128]{2,1,0:T(8,128)S(1)}, u32[]{:S(2)}, u32[]{:S(2)}) async-start(f32[8,128,128]{2,1,0:T(8,128)} %stack.4), calls=%async_computation | async-start | bytes 1048576 | tf_op jit(solution)/shard_map/all_to_all | solution.py:91
  22.9 19.5 %all_gather.13 = f32[3,2048]{1,0:T(4,128)S(1)} all-gather(f32[3,128]{1,0:T(4,128)} %param.15), channel_id=1, replica_groups=mesh['row'=8,'col'=16] {'col'}, dimensions={1}, use_global_device_ids=true | all-gather | bytes 26112 | tf_op jit(solution)/shard_map/all_gather | solution.py:81
  42.3 31.3 %all_gather.14 = f32[3,1024]{1,0:T(4,128)S(1)} all-gather(f32[3,128]{1,0:T(4,128)} %param.15), channel_id=1, replica_groups=mesh['row'=8,'col'=16] {'row'}, dimensions={1}, use_global_device_ids=true | all-gather | bytes 13824 | tf_op jit(solution)/shard_map/all_gather | solution.py:93
  78.1 12.2 %add_convert_fusion.3 = (bf16[16384,128]{1,0:T(8,128)(2,1)}, f32[16384,128]{1,0:T(8,128)}) fusion(f32[128]{0:T(128)S(1)} %get-tuple-element.65, bf16[2,256,128]{2,1,0:T(8,128)(2,1)} %param.21, f32[256]{0:T(256)S(1)} %convert_multiply_fusion, f32[16384]{0:T(1024)S(1)} %get-tuple-element.54), kind=kOutput, calls=%fused_computation.93 | convolution fusion | flops 1109393408 | bytes 12715520 | tf_op jit(solution)/shard_map/dot_general | solution.py:28
  90.4 11.4 %add_convert_fusion.2 = (bf16[16384,128]{1,0:T(8,128)(2,1)}, f32[16384,128]{1,0:T(8,128)}) fusion(f32[128]{0:T(128)S(1)} %get-tuple-element.65, bf16[2,256,128]{2,1,0:T(8,128)(2,1)S(1)} %copy-done.24, f32[16384]{0:T(1024)S(1)} %get-tuple-element.59, f32[256]{0:T(256)S(1)} %convert_multiply_fusion), kind=kOutput, calls=%fused_computation.90 | convolution fusion | flops 1109393408 | bytes 12715520 | tf_op jit(solution)/shard_map/dot_general | solution.py:28
  101.8 6.9 %multiply_reduce_fusion.5 = (f32[128,128]{0,1:T(8,128)S(1)}, f32[128,128,128]{2,1,0:T(8,128)}) fusion(f32[128,128]{0,1:T(8,128)S(1)} %get-tuple-element.45, f32[128,128]{1,0:T(8,128)S(1)} %get-tuple-element.53, bf16[128,128,128]{2,1,0:T(8,128)(2,1)} %bitcast.254, bf16[2,128,128]{2,1,0:T(8,128)(2,1)S(1)} %copy-done.13), kind=kOutput, calls=%fused_computation.87 | convolution fusion | flops 543145984 | bytes 12812288 | tf_op jit(solution)/shard_map/dot_general | solution.py:36
  108.8 6.9 %multiply_reduce_fusion.4 = (f32[128,128]{0,1:T(8,128)S(1)}, f32[128,128,128]{2,1,0:T(8,128)}) fusion(f32[128,128]{0,1:T(8,128)S(1)} %get-tuple-element.44, f32[128,128]{1,0:T(8,128)S(1)} %get-tuple-element.52, bf16[128,128,128]{2,1,0:T(8,128)(2,1)} %bitcast.252, bf16[2,128,128]{2,1,0:T(8,128)(2,1)S(1)} %copy-done.13), kind=kOutput, calls=%fused_computation.86 | convolution fusion | flops 543145984 | bytes 12812288 | tf_op jit(solution)/shard_map/dot_general | solution.py:36
  117.1 11.6 %add_convert_fusion.1 = (bf16[16384,128]{1,0:T(8,128)(2,1)}, f32[16384,128]{1,0:T(8,128)}) fusion(f32[128]{0:T(128)S(1)} %get-tuple-element.64, bf16[2,256,128]{2,1,0:T(8,128)(2,1)S(1)} %copy-done.24, f32[256]{0:T(256)S(1)} %convert_multiply_fusion, f32[16384]{0:T(1024)S(1)} %get-tuple-element.54), kind=kOutput, calls=%fused_computation.89 | convolution fusion | flops 1109393408 | bytes 12715520 | tf_op jit(solution)/shard_map/dot_general | solution.py:28
  128.7 47.3 %reduce-scatter.10.cloned.1.call-done = f32[128,128]{0,1:T(8,128)} async-done(((f32[2048,128]{0,1:T(8,128)}), f32[128,128]{0,1:T(8,128)}) %reduce-scatter.10.cloned.1.call-update) | async-done | bytes 65552 | tf_op jit(solution)/shard_map/reduce_scatter | solution.py:112
  185.1 11.4 %add_convert_fusion = (bf16[16384,128]{1,0:T(8,128)(2,1)}, f32[16384,128]{1,0:T(8,128)}) fusion(f32[128]{0:T(128)S(1)} %get-tuple-element.64, bf16[2,256,128]{2,1,0:T(8,128)(2,1)S(1)} %copy-done.24, f32[16384]{0:T(1024)S(1)} %get-tuple-element.59, f32[256]{0:T(256)S(1)} %convert_multiply_fusion), kind=kOutput, calls=%fused_computation.88 | convolution fusion | flops 1109393408 | bytes 12715520 | tf_op jit(solution)/shard_map/dot_general | solution.py:28
  212.1 61.2 %reduce-scatter.12.cloned.1.call-done = f32[128,128]{0,1:T(8,128)} async-done(((f32[2048,128]{0,1:T(8,128)}), f32[128,128]{0,1:T(8,128)}) %reduce-scatter.12.cloned.1.call-update) | async-done | bytes 65552 | tf_op jit(solution)/shard_map/reduce_scatter | solution.py:112
  276.5 30.8 %all-gather.3.cloned.1.call-done = f32[2048,128]{1,0:T(8,128)} async-done(((f32[128,128]{1,0:T(8,128)}), f32[2048,128]{1,0:T(8,128)}) %all-gather.3.cloned.1.call-update) | async-done | bytes 1048592 | tf_op jit(solution)/shard_map/all_gather | solution.py:128
  319.6 71.7 %reduce-scatter.14.cloned.1.call-done = f32[128,128]{1,0:T(8,128)} async-done(((f32[1024,128]{1,0:T(8,128)}), f32[128,128]{1,0:T(8,128)}) %reduce-scatter.14.cloned.1.call-update) | async-done | bytes 65552 | tf_op jit(solution)/shard_map/reduce_scatter | solution.py:151
  404.9 19.9 %all-gather.5.cloned.1.call-done = f32[2048,128]{1,0:T(8,128)} async-done(((f32[128,128]{1,0:T(8,128)}), f32[2048,128]{1,0:T(8,128)}) %all-gather.5.cloned.1.call-update) | async-done | bytes 1048592 | tf_op jit(solution)/shard_map/all_gather | solution.py:128
  428.8 9.3 %fusion.17 = bf16[16384,128]{1,0:T(8,128)(2,1)S(1)} fusion(bf16[16384,128]{1,0:T(8,128)(2,1)S(1)} %bitcast.258, f32[16384,128]{1,0:T(8,128)} %get-tuple-element.79, bf16[2,128,128]{2,1,0:T(8,128)(2,1)S(1)} %copy-done.13), kind=kOutput, calls=%fused_computation.45 | convolution fusion | flops 566231040 | bytes 16809984 | tf_op jit(solution)/shard_map/transpose(jvp())/dot_general | solution.py:36
  438.1 7.1 %fusion.26 = f32[16384]{0:T(1024)S(1)} fusion(f32[256]{0:T(256)S(1)} %convert_multiply_fusion, f32[16384]{0:T(1024)S(1)} %get-tuple-element.54, bf16[16384,128]{1,0:T(8,128)(2,1)S(1)} %fusion.17, bf16[2,256,128]{2,1,0:T(8,128)(2,1)S(1)} %copy-done.24), kind=kOutput, calls=%fused_computation.54 | convolution fusion | flops 1111474176 | bytes 4391936 | tf_op jit(solution)/shard_map/transpose(jvp())/dot_general | solution.py:28
  445.3 7.1 %fusion.21 = bf16[16384,128]{1,0:T(8,128)(2,1)S(1)} fusion(bf16[16384,128]{1,0:T(8,128)(2,1)S(1)} %bitcast.256, f32[16384,128]{1,0:T(8,128)S(1)} %bitcast.268, bf16[2,128,128]{2,1,0:T(8,128)(2,1)S(1)} %copy-done.13), kind=kOutput, calls=%fused_computation.49 | convolution fusion | flops 566231040 | bytes 16809984 | tf_op jit(solution)/shard_map/transpose(jvp())/dot_general | solution.py:36
  452.4 7.3 %fusion.27 = f32[16384]{0:T(1024)S(1)} fusion(f32[256]{0:T(256)S(1)} %convert_multiply_fusion, f32[16384]{0:T(1024)S(1)} %get-tuple-element.54, bf16[16384,128]{1,0:T(8,128)(2,1)S(1)} %fusion.21, bf16[2,256,128]{2,1,0:T(8,128)(2,1)S(1)} %copy-done.24), kind=kOutput, calls=%fused_computation.55 | convolution fusion | flops 1111474176 | bytes 4391936 | tf_op jit(solution)/shard_map/transpose(jvp())/dot_general | solution.py:28
  467.3 9.2 %fusion.23 = bf16[16384,128]{1,0:T(8,128)(2,1)S(1)} fusion(bf16[16384,128]{1,0:T(8,128)(2,1)S(1)} %bitcast.257, f32[16384,128]{1,0:T(8,128)} %get-tuple-element.75, bf16[2,128,128]{2,1,0:T(8,128)(2,1)S(1)} %copy-done.13), kind=kOutput, calls=%fused_computation.51 | convolution fusion | flops 566231040 | bytes 16809984 | tf_op jit(solution)/shard_map/transpose(jvp())/dot_general | solution.py:36
  476.5 7.3 %fusion.25 = f32[16384]{0:T(1024)S(1)} fusion(f32[16384]{0:T(1024)S(1)} %get-tuple-element.59, f32[256]{0:T(256)S(1)} %convert_multiply_fusion, bf16[16384,128]{1,0:T(8,128)(2,1)S(1)} %fusion.23, bf16[2,256,128]{2,1,0:T(8,128)(2,1)S(1)} %copy-done.24), kind=kOutput, calls=%fused_computation.53 | convolution fusion | flops 1111474176 | bytes 4391936 | tf_op jit(solution)/shard_map/transpose(jvp())/dot_general | solution.py:28
  483.8 9.2 %fusion.19 = bf16[16384,128]{1,0:T(8,128)(2,1)S(1)} fusion(bf16[16384,128]{1,0:T(8,128)(2,1)S(1)} %bitcast.255, f32[16384,128]{1,0:T(8,128)} %get-tuple-element.83, bf16[2,128,128]{2,1,0:T(8,128)(2,1)S(1)} %copy-done.13), kind=kOutput, calls=%fused_computation.47 | convolution fusion | flops 566231040 | bytes 16809984 | tf_op jit(solution)/shard_map/transpose(jvp())/dot_general | solution.py:36
  493.1 7.1 %fusion.24 = f32[16384]{0:T(1024)S(1)} fusion(f32[16384]{0:T(1024)S(1)} %get-tuple-element.59, f32[256]{0:T(256)S(1)} %convert_multiply_fusion, bf16[16384,128]{1,0:T(8,128)(2,1)S(1)} %fusion.19, bf16[2,256,128]{2,1,0:T(8,128)(2,1)S(1)} %copy-done.24), kind=kOutput, calls=%fused_computation.52 | convolution fusion | flops 1111474176 | bytes 4391936 | tf_op jit(solution)/shard_map/transpose(jvp())/dot_general | solution.py:28
  504.7 69.4 %reduce-scatter.18.cloned.1.call-done = f32[128,3]{1,0:T(8,128)} async-done(((f32[1024,3]{1,0:T(8,128)}), f32[128,3]{1,0:T(8,128)}) %reduce-scatter.18.cloned.1.call-update) | async-done | bytes 1552
  575.1 62.7 %reduce-scatter.16.cloned.1.call-done = f32[128,3]{1,0:T(8,128)} async-done(((f32[2048,3]{1,0:T(8,128)}), f32[128,3]{1,0:T(8,128)}) %reduce-scatter.16.cloned.1.call-update) | async-done | bytes 1552
  (157 shorter events, 82.9 us)
Async XLA Ops:
  10.8 91.0 %all-to-all-start = ((f32[8,128,128]{2,1,0:T(8,128)}), f32[8,128,128]{2,1,0:T(8,128)S(1)}, u32[]{:S(2)}, u32[]{:S(2)}) async-start(f32[8,128,128]{2,1,0:T(8,128)} %stack.4), calls=%async_computation | async-start | bytes 1048576 | tf_op jit(solution)/shard_map/all_to_all | solution.py:91
  18.7 157.3 %reduce-scatter.10.cloned.1.call-start = ((), (), s32[]{:S(2)}) async-start(), calls=%async_computation.7 | async-start | bytes 1114112 | tf_op jit(solution)/shard_map/reduce_scatter | solution.py:112
  75.3 15.1 %copy-start.16 = (f32[3,128]{1,0:T(4,128)}, f32[3,128]{1,0:T(4,128)S(1)}, u32[]{:S(2)}) copy-start(f32[3,128]{1,0:T(4,128)S(1)} %get-tuple-element.60) | copy-start | bytes 4612
  75.3 15.0 %copy-start.18 = (f32[3,128]{1,0:T(4,128)}, f32[3,128]{1,0:T(4,128)S(1)}, u32[]{:S(2)}) copy-start(f32[3,128]{1,0:T(4,128)S(1)} %get-tuple-element.62) | copy-start | bytes 4612
  75.3 15.0 %copy-start.22 = (f32[3,128]{1,0:T(4,128)}, f32[3,128]{1,0:T(4,128)S(1)}, u32[]{:S(2)}) copy-start(f32[3,128]{1,0:T(4,128)S(1)} %get-tuple-element.63) | copy-start | bytes 4612
  75.4 14.9 %copy-start.7 = (f32[128,128]{1,0:T(8,128)}, f32[128,128]{1,0:T(8,128)S(1)}, u32[]{:S(2)}) copy-start(f32[128,128]{1,0:T(8,128)S(1)} %fusion.74) | copy-start | bytes 196612
  76.0 14.4 %copy-start.9 = (f32[128,128]{1,0:T(8,128)}, f32[128,128]{1,0:T(8,128)S(1)}, u32[]{:S(2)}) copy-start(f32[128,128]{1,0:T(8,128)S(1)} %fusion.75) | copy-start | bytes 196612
  117.0 59.0 %copy-start.11 = (f32[2,128,128]{2,1,0:T(8,128)S(1)}, f32[2,128,128]{2,1,0:T(8,128)}, u32[]{:S(2)}) copy-start(f32[2,128,128]{2,1,0:T(8,128)} %param.24) | copy-start | bytes 393220
  117.0 60.1 %copy-start.14 = (f32[2,128,128]{2,1,0:T(8,128)S(1)}, f32[2,128,128]{2,1,0:T(8,128)}, u32[]{:S(2)}) copy-start(f32[2,128,128]{2,1,0:T(8,128)} %param.25) | copy-start | bytes 393220
  117.0 60.3 %copy-start.12 = (f32[2,128,128]{2,1,0:T(8,128)S(1)}, f32[2,128,128]{2,1,0:T(8,128)}, u32[]{:S(2)}) copy-start(f32[2,128,128]{2,1,0:T(8,128)} %param.20) | copy-start | bytes 393220
  178.4 18.0 %all-to-all-start.1 = ((f32[8,128,128]{2,1,0:T(8,128)}), f32[8,128,128]{2,1,0:T(8,128)S(1)}, u32[]{:S(2)}, u32[]{:S(2)}) async-start(f32[8,128,128]{2,1,0:T(8,128)} %stack.5), calls=%async_computation.2 | async-start | bytes 1048576 | tf_op jit(solution)/shard_map/all_to_all | solution.py:91
  185.0 88.2 %reduce-scatter.12.cloned.1.call-start = ((), (), s32[]{:S(2)}) async-start(), calls=%async_computation.8 | async-start | bytes 1114112 | tf_op jit(solution)/shard_map/reduce_scatter | solution.py:112
  203.3 71.3 %copy-start.15 = (f32[128,64]{0,1:T(8,128)S(1)}, f32[128,64]{0,1:T(8,128)}, u32[]{:S(2)}) copy-start(f32[128,64]{0,1:T(8,128)} %param.26) | copy-start | bytes 98308
  203.3 71.5 %copy-start.25 = (f32[64]{0:T(128)S(1)}, f32[64]{0:T(128)}, u32[]{:S(2)}) copy-start(f32[64]{0:T(128)} %param.27) | copy-start | bytes 772
  211.6 95.7 %all-gather.3.cloned.1.call-start = ((), (), s32[]{:S(2)}) async-start(), calls=%async_computation.9 | async-start | bytes 1114112 | tf_op jit(solution)/shard_map/all_gather | solution.py:128
  276.4 114.8 %reduce-scatter.14.cloned.1.call-start = ((), (), s32[]{:S(2)}) async-start(), calls=%async_computation.10 | async-start | bytes 589824 | tf_op jit(solution)/shard_map/reduce_scatter | solution.py:151
  319.5 105.3 %all-gather.5.cloned.1.call-start = ((), (), s32[]{:S(2)}) async-start(), calls=%async_computation.11 | async-start | bytes 1114112 | tf_op jit(solution)/shard_map/all_gather | solution.py:128
  393.5 180.6 %reduce-scatter.18.cloned.1.call-start = ((), (), s32[]{:S(2)}) async-start(), calls=%async_computation.13 | async-start | bytes 589824
  425.7 19.5 %slice-start.4 = ((s8[8388608]{0:T(1024)(128)(4,1)}), s8[4194304]{0:T(1024)(128)(4,1)S(1)}, s32[]{:S(2)}) async-start(s8[8388608]{0:T(1024)(128)(4,1)} %bitcast.267), calls=%async_computation.18 | async-start | bytes 8388608
  428.8 16.5 %slice-start.5 = ((s8[8388608]{0:T(1024)(128)(4,1)}), s8[4194304]{0:T(1024)(128)(4,1)S(1)}, s32[]{:S(2)}) async-start(s8[8388608]{0:T(1024)(128)(4,1)} %bitcast.267), calls=%async_computation.19 | async-start | bytes 8388608
  438.1 21.6 %slice-start.2 = ((s8[8388608]{0:T(1024)(128)(4,1)}), s8[4194304]{0:T(1024)(128)(4,1)S(1)}, s32[]{:S(2)}) async-start(s8[8388608]{0:T(1024)(128)(4,1)} %bitcast.249), calls=%async_computation.16 | async-start | bytes 8388608
  445.2 14.5 %slice-start.3 = ((s8[8388608]{0:T(1024)(128)(4,1)}), s8[4194304]{0:T(1024)(128)(4,1)S(1)}, s32[]{:S(2)}) async-start(s8[8388608]{0:T(1024)(128)(4,1)} %bitcast.249), calls=%async_computation.17 | async-start | bytes 8388608
  493.1 146.2 %copy-start.1 = (f32[100,128]{1,0:T(8,128)S(1)}, f32[100,128]{1,0:T(8,128)}, u32[]{:S(2)}) copy-start(f32[100,128]{1,0:T(8,128)} %param.19) | copy-start | bytes 153604
  502.5 135.3 %reduce-scatter.16.cloned.1.call-start = ((), (), s32[]{:S(2)}) async-start(), calls=%async_computation.12 | async-start | bytes 1114112
  (17 other events, 89.7 us)
Sparse Core Ops, SparseCore 0:
  117.1 58.7 reduce-scatter.9
  211.7 61.4 reduce-scatter.11
  276.5 30.6 all-gather.2
  319.6 71.5 reduce-scatter.13
  393.7 31.0 all-gather.4
  502.6 71.4 reduce-scatter.17
  576.5 61.2 reduce-scatter.15
